TPU v7x, 128 devices: a whole 4x4x4 slice. The times are simulated.
128 devices in a mesh: feat: 8 (over x, z_lo), seq: 16 (over z_hi, y, core).
Axes of the slice: x: 4, y: 4, z: 4 (z_hi: 2, z_lo: 2; z = z_hi * 2 + z_lo), core: 2. Of those that a mesh axis runs over, the one named last changes fastest.
Arguments:
- tokens: bfloat16 [8192, 8192], P('seq', 'feat'), may hold values from -6 to 6
- block_weights: bfloat16 [28672, 512], P('feat'), may hold values from -0.25 to 0.25
- left_factor: bfloat16 [28672, 256], P('feat'), may hold values from -0.09375 to 0.09375
- right_factor: bfloat16 [8192, 256], P('feat'), may hold values from -0.0625 to 0.0625
- pattern: int32 [224, 4], P('feat'), may hold values from 0 to 63, as said below
- cotangent: bfloat16 [8192, 28672], P('seq', 'feat'), may hold values from -6 to 6
Outputs:
- activated: bfloat16 [8192, 28672], P('seq', 'feat')
- grad_input: bfloat16 [16, 512, 8192], P('seq', 'feat')
- grad_blocks: float32 [28672, 512], P(('feat', 'seq'))
- grad_left: float32 [28672, 256], P(('feat', 'seq'))
- grad_right: float32 [8192, 256], P(('feat', 'seq'))
Inputs may be any that keep to these rules, and one draw needn't show every extreme that they name: For block row f, pattern[f, 0] // 8 equals (f * 8) // 224, and pattern[f, j] = pattern[f, 0] XOR ((64) >> j) for 1 <= j < 4.
All inputs are finite; a program needn't handle non-finite values.
Results may differ from a plain program's by a relative error of at most 0.0051.
Values may be sent and summed in bfloat16 or wider, within the bound.
A program may use at most 192 MiB of HBM per device.

v0:
```python
import math
import jax
import jax.numpy as jnp
from jax import lax
from jax.sharding import PartitionSpec as P

BLK = 128
LEVELS = 4


def from_partner(value, axis, distance):
    mask = 2**distance
    pairs = [(source, source ^ mask) for source in range(lax.axis_size(axis))]
    return lax.ppermute(value, axis, pairs)


def activation(values):
    return jax.nn.gelu(values, approximate=True)


def partner_bit(stride, local_blocks):
    return (stride // local_blocks).bit_length() - 1


def local(tokens, block_weights, left_factor, right_factor, pattern, cotangent):
    tok_rows, local_width = tokens.shape
    feat_count = lax.axis_size("feat")
    seq_count = lax.axis_size("seq")
    norm_scale = 1.0 / math.sqrt(tok_rows * seq_count)
    local_blocks = local_width // BLK
    all_blocks = local_blocks * feat_count
    row_blocks = pattern.shape[0]
    out_rows = block_weights.shape[0]
    weight_blocks = block_weights.reshape(row_blocks, BLK, LEVELS, BLK)
    strides = [0] + [all_blocks >> level for level in range(1, LEVELS)]
    pieces = []
    for level in range(LEVELS):
        bit_index = partner_bit(strides[level], local_blocks) if level > 0 else -1
        source = tokens if bit_index < 0 else from_partner(tokens, "feat", bit_index)
        local_ids = pattern[:, level] % local_blocks
        pieces.append(jnp.take(source.reshape(tok_rows, local_blocks, BLK), local_ids, axis=1))
    picked = jnp.stack(pieces, axis=2)
    sparse = jnp.einsum("tfli,foli->tfo", picked, weight_blocks, preferred_element_type=jnp.float32)
    latent_part = jnp.dot(tokens, right_factor, preferred_element_type=jnp.float32)
    latent = lax.psum(latent_part, "feat").astype(jnp.bfloat16)
    pre = sparse.reshape(tok_rows, out_rows) + jnp.einsum(
        "tr,or->to", latent, left_factor, preferred_element_type=jnp.float32
    )
    activated, slope = jax.vjp(activation, pre)
    grad_pre = slope(cotangent.astype(jnp.float32))[0].astype(jnp.bfloat16)
    back_part = jnp.einsum("to,or->tr", grad_pre, left_factor, preferred_element_type=jnp.float32)
    back_latent = lax.psum(back_part, "feat").astype(jnp.bfloat16)
    low_rank = jnp.einsum(
        "tr,ir->ti", back_latent, right_factor, preferred_element_type=jnp.float32
    )
    grad_rows = grad_pre.reshape(tok_rows, row_blocks, BLK)
    spread = jnp.einsum(
        "tfo,foli->tfli", grad_rows, weight_blocks, preferred_element_type=jnp.float32
    )
    summed_grad = low_rank
    for level in range(LEVELS):
        bit_index = partner_bit(strides[level], local_blocks) if level > 0 else -1
        local_ids = pattern[:, level] % local_blocks
        level_term = (
            jnp.zeros((tok_rows, local_blocks, BLK), jnp.float32)
            .at[:, local_ids, :]
            .add(spread[:, :, level, :])
        )
        level_term = level_term.reshape(tok_rows, local_width)
        if bit_index >= 0:
            level_term = from_partner(level_term, "feat", bit_index)
        summed_grad = summed_grad + level_term
    local_grad = summed_grad.astype(jnp.bfloat16)
    regrouped = lax.all_to_all(local_grad, "feat", split_axis=0, concat_axis=1, tiled=True)
    grad_input = regrouped.reshape(1, tok_rows // feat_count, feat_count * local_width)
    window = min(out_rows // seq_count * lax.axis_size("seq") // BLK + 2, row_blocks)
    product = jnp.einsum("tfo,tfli->foli", grad_rows, picked, preferred_element_type=jnp.float32)
    product = product.reshape(window * BLK, LEVELS * BLK) * norm_scale
    grad_blocks = lax.psum_scatter(product, "seq", scatter_dimension=0, tiled=True)
    left_term = (
        jnp.einsum("to,tr->or", grad_pre, latent, preferred_element_type=jnp.float32) * norm_scale
    )
    right_term = (
        jnp.einsum("ti,tr->ir", tokens, back_latent, preferred_element_type=jnp.float32)
        * norm_scale
    )
    grad_left, grad_right = (
        lax.psum_scatter(left_term, "seq", scatter_dimension=0, tiled=True),
        lax.psum_scatter(right_term, "seq", scatter_dimension=0, tiled=True),
    )
    return (activated.astype(jnp.bfloat16), grad_input, grad_blocks, grad_left, grad_right)


def solution(mesh):
    in_specs = (
        P("seq", "feat"),
        P("feat", None),
        P("feat", None),
        P("feat", None),
        P("feat", None),
        P("seq", "feat"),
    )
    out_specs = (
        P("seq", "feat"),
        P("seq", "feat", None),
        P(("feat", "seq"), None),
        P(("feat", "seq"), None),
        P(("feat", "seq"), None),
    )
    return jax.shard_map(local, mesh=mesh, in_specs=in_specs, out_specs=out_specs, check_vma=False)
```

profile of v0, /device:TPU:0, one launch (start us, length us, event | category | flops | bytes accessed | tf_op | source)
XLA Modules:
  0.0 451.5 jit_solution(5003942331406243700)
XLA Ops:
  19.3 6.3 %reshape.62 = bf16[28,128,4,128]{3,2,1,0:T(4,128)(2,1)} reshape(bf16[3584,512]{1,0:T(8,128)(2,1)} %param.9) | data formatting | bytes 7340032 | tf_op jit(solution)/shard_map/reshape | solution.py:34
  28.5 61.9 %all-reduce.2 = bf16[512,256]{1,0:T(8,128)(2,1)} all-reduce(f32[512,256]{1,0:T(8,128)S(1)} %fusion.36), channel_id=1, replica_groups=mesh['feat'=8,'seq'=16] {'feat'}, use_global_device_ids=true, to_apply=%region_0.2 | all-reduce | flops 131072 | bytes 786432 | tf_op jit(solution)/shard_map/psum | solution.py:45
  99.5 4.2 gather_fusion.3
  106.6 5.8 %select_bitcast_fusion = (bf16[512,28,1,128]{3,0,2,1:T(8,128)(2,1)S(1)}, bf16[512,28,1,128]{3,0,2,1:T(8,128)(2,1)}) fusion(bf16[28,512,128]{2,1,0:T(8,128)(2,1)} %gather_fusion.3, pred[28]{0:T(512)(128)(4,1)S(1)} %get-tuple-element.46, bf16[28,512,128]{2,1,0:T(8,128)(2,1)} %gather_fusion.2, pred[28]{0:T(512)(128)(4,1)S(1)} %get-tuple-element.48), kind=kLoop, calls=%fused_computation.32 | loop fusion | flops 3670016 | bytes 14680120 | tf_op jit(solution)/shard_map/stack | solution.py:42
  112.6 4.1 select_bitcast_fusion.2
  117.3 9.7 %fusion.11 = f32[28,512,128,1]{1,2,3,0:T(8,128)} fusion(bf16[28,128,4,128]{3,2,1,0:T(4,128)(2,1)S(1)} %copy-done.5, bf16[512,28,1,128]{3,0,2,1:T(8,128)(2,1)S(1)} %get-tuple-element.50, bf16[512,28,1,128]{3,0,2,1:T(8,128)(2,1)} %get-tuple-element.51, bf16[512,28,1,128]{3,0,2,1:T(8,128)(2,1)} %get-tuple-element.52, ...), kind=kOutput, calls=%fused_computation.38 | convolution fusion | flops 1901068288 | bytes 25690112 | tf_op jit(solution)/shard_map/tfli,foli->tfo/dot_general | solution.py:43
  127.0 8.5 %copy.63 = f32[512,3584]{1,0:T(8,128)} copy(f32[512,3584]{0,1:T(8,128)} %bitcast.128) | data formatting | bytes 14680064 | tf_op jit(solution)/shard_map/reshape | solution.py:46
  135.5 10.3 %fusion.2 = (bf16[512,3584]{1,0:T(8,128)(2,1)S(1)}, bf16[512,3584]{1,0:T(8,128)(2,1)}) fusion(bf16[512,3584]{1,0:T(8,128)(2,1)} %param.13, f32[512,3584]{1,0:T(8,128)} %copy.63, bf16[512,256]{1,0:T(8,128)(2,1)S(1)} %copy-done.10, bf16[3584,256]{1,0:T(8,128)(2,1)S(1)} %copy-done), kind=kOutput, calls=%fused_computation.16 | convolution fusion | flops 983564288 | bytes 20447232 | tf_op jit(solution)/shard_map/tr,or->to/dot_general | solution.py:46
  149.6 40.0 %all-reduce.3 = bf16[512,256]{1,0:T(8,128)(2,1)S(1)} all-reduce(f32[512,256]{1,0:T(8,128)} %fusion.37), channel_id=1, replica_groups=mesh['feat'=8,'seq'=16] {'feat'}, use_global_device_ids=true, to_apply=%region_1.3 | all-reduce | flops 131072 | bytes 786432 | tf_op jit(solution)/shard_map/psum | solution.py:52
  191.4 5.0 %convolution_multiply_fusion = f32[3584,256]{1,0:T(8,128)} fusion(bf16[512,3584]{1,0:T(8,128)(2,1)} %copy-done.7, bf16[512,256]{1,0:T(8,128)(2,1)S(1)} %copy-done.10), kind=kOutput, calls=%fused_computation.31 | convolution fusion | flops 940441600 | bytes 7602176 | tf_op jit(solution)/shard_map/to,tr->or/dot_general | solution.py:81
  196.5 6.0 %copy.64 = bf16[512,3584]{0,1:T(8,128)(2,1)} copy(bf16[512,3584]{1,0:T(8,128)(2,1)} %copy-done.7) | data formatting | bytes 7340032 | tf_op jit(solution)/shard_map/convert_element_type | solution.py:50
  202.5 10.9 %broadcast_multiply_fusion = f32[28,128,4,128]{3,1,2,0:T(8,128)} fusion(bf16[512,28,128,1]{0,2,3,1:T(8,128)(2,1)} %bitcast.126, bf16[512,28,1,128]{3,0,2,1:T(8,128)(2,1)} %copy-done.8, bf16[512,28,1,128]{3,0,2,1:T(8,128)(2,1)} %get-tuple-element.51, bf16[512,28,1,128]{3,0,2,1:T(8,128)(2,1)} %get-tuple-element.52, ...), kind=kOutput, calls=%fused_computation.36 | convolution fusion | flops 1939603456 | bytes 25690112 | tf_op jit(solution)/shard_map/tfo,tfli->foli/dot_general | solution.py:77
  213.4 9.2 %copy.72 = f32[28,128,4,128]{3,2,1,0:T(4,128)S(1)} copy(f32[28,128,4,128]{3,1,2,0:T(8,128)} %broadcast_multiply_fusion) | data formatting | bytes 14680064 | tf_op jit(solution)/shard_map/mul | solution.py:78
  226.4 17.0 %convolution_bitcast_fusion = f32[512,28,4,128]{3,0,2,1:T(8,128)} fusion(bf16[512,28,128,1]{0,2,3,1:T(8,128)(2,1)} %bitcast.127, bf16[28,128,4,128]{3,2,1,0:T(4,128)(2,1)} %reshape.62), kind=kOutput, calls=%fused_computation.9 | convolution fusion | flops 1879048192 | bytes 36700160 | tf_op jit(solution)/shard_map/tfo,foli->tfli/dot_general | solution.py:57
  243.4 20.2 %slice_bitcast_fusion.3 = (f32[28,512,128]{2,1,0:T(8,128)}, f32[28,512,128]{2,1,0:T(8,128)}, f32[28,512,128]{2,1,0:T(8,128)}, f32[28,512,128]{2,1,0:T(8,128)}) fusion(f32[512,28,4,128]{3,0,2,1:T(8,128)} %convolution_bitcast_fusion), kind=kLoop, calls=%fused_computation.28 | loop fusion | bytes 58720256 | tf_op jit(solution)/shard_map/squeeze | solution.py:67
  265.1 18.0 %scatter_fusion.1 = f32[512,8,128]{2,0,1:T(8,128)} fusion(f32[512,8,128]{2,0,1:T(8,128)} %broadcast.93.clone.2, s32[28]{0:T(128)S(1)} %get-tuple-element.41, f32[28,512,128]{2,1,0:T(8,128)} %get-tuple-element.37), kind=kCustom, calls=%fused_computation.5 | custom fusion | flops 1835008 | bytes 22020208 | tf_op jit(solution)/shard_map/scatter-add | solution.py:67
  287.9 17.7 %scatter_fusion.2 = f32[512,8,128]{2,0,1:T(8,128)} fusion(f32[512,8,128]{2,0,1:T(8,128)} %broadcast.93.clone.1, s32[28]{0:T(128)S(1)} %get-tuple-element.42, f32[28,512,128]{2,1,0:T(8,128)} %get-tuple-element.36), kind=kCustom, calls=%fused_computation.6 | custom fusion | flops 1835008 | bytes 22020208 | tf_op jit(solution)/shard_map/scatter-add | solution.py:67
  311.3 17.8 %scatter_fusion.3 = f32[512,8,128]{2,0,1:T(8,128)} fusion(f32[512,8,128]{2,0,1:T(8,128)} %broadcast.93.clone, s32[28]{0:T(128)S(1)} %get-tuple-element.43, f32[28,512,128]{2,1,0:T(8,128)} %get-tuple-element.35), kind=kCustom, calls=%fused_computation.7 | custom fusion | flops 1835008 | bytes 22020208 | tf_op jit(solution)/shard_map/scatter-add | solution.py:67
  335.3 17.7 %scatter_fusion = f32[512,8,128]{2,0,1:T(8,128)} fusion(f32[512,8,128]{2,0,1:T(8,128)} %broadcast.93.clone.3, s32[28]{0:T(128)S(1)} %get-tuple-element.40, f32[28,512,128]{2,1,0:T(8,128)} %get-tuple-element.34), kind=kCustom, calls=%fused_computation.4 | custom fusion | flops 1835008 | bytes 22020208 | tf_op jit(solution)/shard_map/scatter-add | solution.py:67
  353.0 12.0 %collective-permute-done.4 = f32[512,1024]{1,0:T(8,128)} collective-permute-done((f32[512,1024]{1,0:T(8,128)}, f32[512,1024]{1,0:T(8,128)}, u32[]{:S(2)}, u32[]{:S(2)}) %collective-permute-start.4) | collective-permute-done | bytes 2097184 | tf_op jit(solution)/shard_map/ppermute | solution.py:14
  365.0 9.2 %collective-permute-done.5 = f32[512,1024]{1,0:T(8,128)} collective-permute-done((f32[512,1024]{1,0:T(8,128)}, f32[512,1024]{1,0:T(8,128)}, u32[]{:S(2)}, u32[]{:S(2)}) %collective-permute-start.5) | collective-permute-done | bytes 2097184 | tf_op jit(solution)/shard_map/ppermute | solution.py:14
  374.2 4.2 fusion.16
  378.4 15.6 %all_to_all.16 = bf16[8,64,1024]{2,1,0:T(8,128)(2,1)S(1)} all-to-all(bf16[8,64,1024]{2,1,0:T(8,128)(2,1)S(1)} %bitcast.129), channel_id=1, replica_groups=mesh['feat'=8,'seq'=16] {'feat'}, dimensions={0} | all-to-all | bytes 2097152 | tf_op jit(solution)/shard_map/all_to_all | solution.py:74
  395.9 49.1 %reduce-scatter.6.cloned.1.call-done = f32[224,512]{1,0:T(8,128)} async-done(((f32[3584,512]{1,0:T(8,128)}), f32[224,512]{1,0:T(8,128)}) %reduce-scatter.6.cloned.1.call-update) | async-done | bytes 458768 | tf_op jit(solution)/shard_map/reduce_scatter | solution.py:79
  (70 shorter events, 57.2 us)
Async XLA Ops:
  7.2 128.3 %copy-start = (bf16[3584,256]{1,0:T(8,128)(2,1)S(1)}, bf16[3584,256]{1,0:T(8,128)(2,1)}, u32[]{:S(2)}) copy-start(bf16[3584,256]{1,0:T(8,128)(2,1)} %param.10) | copy-start | bytes 5505028
  7.2 10.5 %copy-start.11 = (s32[28,4]{0,1:T(4,128)S(1)}, s32[28,4]{0,1:T(4,128)}, u32[]{:S(2)}) copy-start(s32[28,4]{0,1:T(4,128)} %param.12) | copy-start | bytes 1348
  7.2 388.7 %reduce-scatter.10.cloned.1.call-start = ((), (), s32[]{:S(2)}) async-start(), calls=%async_computation.6 | async-start | bytes 1114112
  9.6 80.8 %collective-permute-start.1 = (bf16[512,1024]{0,1:T(8,128)(2,1)}, bf16[512,1024]{0,1:T(8,128)(2,1)}, u32[]{:S(2)}, u32[]{:S(2)}) collective-permute-start(bf16[512,1024]{0,1:T(8,128)(2,1)} %copy.54), channel_id=1, source_target_pairs={{0,32},{16,48},{32,0},{48,16},{64,96},{80,112},{96,64},{112,80},{1... | collective-permute-start | bytes 3145736 | tf_op jit(solution)/shard_map/ppermute | solution.py:14
  11.2 80.9 %collective-permute-start.2 = (bf16[512,1024]{0,1:T(8,128)(2,1)}, bf16[512,1024]{0,1:T(8,128)(2,1)}, u32[]{:S(2)}, u32[]{:S(2)}) collective-permute-start(bf16[512,1024]{0,1:T(8,128)(2,1)} %copy.54), channel_id=1, source_target_pairs={{0,16},{16,0},{32,48},{48,32},{64,80},{80,64},{96,112},{112,96},{1... | collective-permute-start | bytes 3145736 | tf_op jit(solution)/shard_map/ppermute | solution.py:14
  13.1 81.2 %collective-permute-start = (bf16[512,1024]{0,1:T(8,128)(2,1)}, bf16[512,1024]{0,1:T(8,128)(2,1)}, u32[]{:S(2)}, u32[]{:S(2)}) collective-permute-start(bf16[512,1024]{0,1:T(8,128)(2,1)} %copy.54), channel_id=1, source_target_pairs={{0,64},{16,80},{32,96},{48,112},{64,0},{80,16},{96,32},{112,48},{1... | collective-permute-start | bytes 3145736 | tf_op jit(solution)/shard_map/ppermute | solution.py:14
  99.5 4.2 copy-start.2
  106.6 5.8 %copy-start.3 = (bf16[28,512,128]{2,1,0:T(8,128)(2,1)S(1)}, bf16[28,512,128]{2,1,0:T(8,128)(2,1)}, u32[]{:S(2)}) copy-start(bf16[28,512,128]{2,1,0:T(8,128)(2,1)} %gather_fusion) | copy-start | bytes 11010052
  106.6 6.0 %copy-start.4 = (bf16[28,512,128]{2,1,0:T(8,128)(2,1)S(1)}, bf16[28,512,128]{2,1,0:T(8,128)(2,1)}, u32[]{:S(2)}) copy-start(bf16[28,512,128]{2,1,0:T(8,128)(2,1)} %gather_fusion.1) | copy-start | bytes 11010052
  112.4 4.9 %copy-start.8 = (bf16[512,28,1,128]{3,0,2,1:T(8,128)(2,1)}, bf16[512,28,1,128]{3,0,2,1:T(8,128)(2,1)S(1)}, u32[]{:S(2)}) copy-start(bf16[512,28,1,128]{3,0,2,1:T(8,128)(2,1)S(1)} %get-tuple-element.50) | copy-start | bytes 11010052
  112.6 4.7 %copy-start.5 = (bf16[28,128,4,128]{3,2,1,0:T(4,128)(2,1)S(1)}, bf16[28,128,4,128]{3,2,1,0:T(4,128)(2,1)}, u32[]{:S(2)}) copy-start(bf16[28,128,4,128]{3,2,1,0:T(4,128)(2,1)} %reshape.62) | copy-start | bytes 11010052
  127.0 8.5 %copy-start.10 = (bf16[512,256]{1,0:T(8,128)(2,1)S(1)}, bf16[512,256]{1,0:T(8,128)(2,1)}, u32[]{:S(2)}) copy-start(bf16[512,256]{1,0:T(8,128)(2,1)} %all-reduce.2) | copy-start | bytes 786436
  145.8 1.8 copy-start.7
  147.7 41.9 %copy-start.6 = (bf16[512,1024]{1,0:T(8,128)(2,1)S(1)}, bf16[512,1024]{1,0:T(8,128)(2,1)}, u32[]{:S(2)}) copy-start(bf16[512,1024]{1,0:T(8,128)(2,1)} %param.8) | copy-start | bytes 3145732
  191.3 204.6 %reduce-scatter.8.cloned.1.call-start = ((), (), s32[]{:S(2)}) async-start(), calls=%async_computation.5 | async-start | bytes 3899392 | tf_op jit(solution)/shard_map/reduce_scatter | solution.py:88
  196.4 248.6 %reduce-scatter.6.cloned.1.call-start = ((), (), s32[]{:S(2)}) async-start(), calls=%async_computation.4 | async-start | bytes 7798784 | tf_op jit(solution)/shard_map/reduce_scatter | solution.py:79
  286.4 66.6 %collective-permute-start.3 = (f32[512,1024]{1,0:T(8,128)}, f32[512,1024]{1,0:T(8,128)}, u32[]{:S(2)}, u32[]{:S(2)}) collective-permute-start(f32[512,1024]{1,0:T(8,128)} %copy_bitcast_fusion.3), channel_id=1, source_target_pairs={{0,64},{16,80},{32,96},{48,112},{64,0},{80,16},{96,32},{112,48},{1... | collective-permute-start | bytes 6291464 | tf_op jit(solution)/shard_map/ppermute | solution.py:14
  308.8 56.3 %collective-permute-start.4 = (f32[512,1024]{1,0:T(8,128)}, f32[512,1024]{1,0:T(8,128)}, u32[]{:S(2)}, u32[]{:S(2)}) collective-permute-start(f32[512,1024]{1,0:T(8,128)} %copy_bitcast_fusion.2), channel_id=1, source_target_pairs={{0,32},{16,48},{32,0},{48,16},{64,96},{80,112},{96,64},{112,80},{1... | collective-permute-start | bytes 6291464 | tf_op jit(solution)/shard_map/ppermute | solution.py:14
  332.3 41.9 %collective-permute-start.5 = (f32[512,1024]{1,0:T(8,128)}, f32[512,1024]{1,0:T(8,128)}, u32[]{:S(2)}, u32[]{:S(2)}) collective-permute-start(f32[512,1024]{1,0:T(8,128)} %copy_bitcast_fusion.1), channel_id=1, source_target_pairs={{0,16},{16,0},{32,48},{48,32},{64,80},{80,64},{96,112},{112,96},{1... | collective-permute-start | bytes 6291464 | tf_op jit(solution)/shard_map/ppermute | solution.py:14
  335.3 38.9 %copy-start.9 = (bf16[1024,256]{1,0:T(8,128)(2,1)S(1)}, bf16[1024,256]{1,0:T(8,128)(2,1)}, u32[]{:S(2)}) copy-start(bf16[1024,256]{1,0:T(8,128)(2,1)} %param.11) | copy-start | bytes 1572868
  374.2 70.8 %copy-start.1 = (bf16[3584,256]{1,0:T(8,128)(2,1)S(1)}, bf16[3584,256]{1,0:T(8,128)(2,1)}, u32[]{:S(2)}) copy-start(bf16[3584,256]{1,0:T(8,128)(2,1)} %param.10) | copy-start | bytes 5505028
Sparse Core Ops, SparseCore 0:
  191.4 66.7 reduce-scatter.9
  263.4 77.6 reduce-scatter.7
  346.5 98.4 reduce-scatter.5
where the time goes:
time: 453 us; the launch traced here: 452 us
  blocking collectives  117 us (26%)
  local copies, waits for them, and re-layouts  98.5 us (22%)
  other arithmetic  81.2 us (18%)
  waiting for transfers between devices  70.4 us (16%)
  matrix products  61.3 us (14%)
  between operations  13.9 us (3%)
  starting transfers between devices  8.89 us (2%)
    scatter-add x4, other arithmetic, local(): level_term = jnp.zeros((tok_rows, local_blocks, BLK), jnp.float32).at[:,...  71.2 us
    psum x1, blocking collectives, local(): latent = lax.psum(latent_part, 'feat').astype(jnp.bfloat16)  61.9 us
    reduce_scatter x1, waiting for transfers between devices, local(): lax.psum_scatter(product, 'seq', scatter_dimension=0, tiled=True)  49.1 us
    psum x1, blocking collectives, local(): back_latent = lax.psum(back_part, 'feat').astype(jnp.bfloat16)  40 us
    ppermute x6, waiting for transfers between devices, from_partner(): return lax.ppermute(value, axis, pairs)  21.2 us
    squeeze x1, local copies, waits for them, and re-layouts, local(): spread[:, :, level, :]  20.2 us
    dot_general x1, matrix products, local(): jnp.einsum('tfo,foli->tfli', grad_rows, weight_blocks, preferred_element_...  17 us
    all_to_all x1, blocking collectives, local(): lax.all_to_all(local_grad, 'feat', split_axis=0, concat_axis=1, tiled=True)  15.6 us
  transfers between devices with their start and end apart: 9, of which 3 were waited for; matrix products, arithmetic and copies ran while one was open for 40% of the time, Pallas kernels for 0%

commit v1 on v0

--- a/solution.py
+++ b/solution.py
@@ -3,6 +3,7 @@
 import jax.numpy as jnp
 from jax import lax
 from jax.sharding import PartitionSpec as P
+from jax.lax import all_gather
 
 BLK = 128
 LEVELS = 4
@@ -49,7 +50,8 @@
     activated, slope = jax.vjp(activation, pre)
     grad_pre = slope(cotangent.astype(jnp.float32))[0].astype(jnp.bfloat16)
     back_part = jnp.einsum("to,or->tr", grad_pre, left_factor, preferred_element_type=jnp.float32)
-    back_latent = lax.psum(back_part, "feat").astype(jnp.bfloat16)
+    _change_task = lambda t0, row_axis: jnp.sum(all_gather(t0, row_axis), axis=0)
+    back_latent = _change_task(back_part, "feat").astype(jnp.bfloat16)
     low_rank = jnp.einsum(
         "tr,ir->ti", back_latent, right_factor, preferred_element_type=jnp.float32
     )

time: 453 us -> 476 us (1.051)
  waiting for transfers between devices: 70.4 us -> 125 us
  blocking collectives: 117 us -> 79.9 us
    all_gather x0 -> x1, waiting for transfers between devices: none -> 92.5 us  [local(): all_gather(t0, row_axis)]
    reduce_scatter x1, waiting for transfers between devices: 49.1 us -> 0.01 us  [local(): lax.psum_scatter(product, 'seq', scatter_dimension=0, tiled=True)]
    psum x1 -> x0, blocking collectives: 40 us -> none  [local(): back_latent = lax.psum(back_part, 'feat').astype(jnp.bfloat16)]
    ppermute x6, waiting for transfers between devices: 21.2 us -> 32.3 us  [from_partner(): return lax.ppermute(value, axis, pairs)]
  transfers between devices with their start and end apart: 9 -> 10, of which waited for: 3 -> 3; matrix products, arithmetic and copies ran while one was open for 40% -> 39% of each run, Pallas kernels for 0% -> 0%
where the time goes in v1:
time: 476 us; the launch traced here: 475 us
  waiting for transfers between devices  125 us (26%)
  local copies, waits for them, and re-layouts  98.5 us (21%)
  other arithmetic  84.4 us (18%)
  blocking collectives  79.9 us (17%)
  matrix products  60.9 us (13%)
  between operations  15.8 us (3%)
  starting transfers between devices  10.2 us (2%)
    all_gather x1, waiting for transfers between devices, local(): all_gather(t0, row_axis)  92.5 us
    scatter-add x4, other arithmetic, local(): level_term = jnp.zeros((tok_rows, local_blocks, BLK), jnp.float32).at[:,...  71.9 us
    psum x1, blocking collectives, local(): latent = lax.psum(latent_part, 'feat').astype(jnp.bfloat16)  61.9 us
    ppermute x6, waiting for transfers between devices, from_partner(): return lax.ppermute(value, axis, pairs)  32.3 us
    squeeze x1, local copies, waits for them, and re-layouts, local(): spread[:, :, level, :]  20.2 us
    all_to_all x1, blocking collectives, local(): lax.all_to_all(local_grad, 'feat', split_axis=0, concat_axis=1, tiled=True)  18 us
    dot_general x1, matrix products, local(): jnp.einsum('tfo,foli->tfli', grad_rows, weight_blocks, preferred_element_...  17 us
    gather x4, local copies, waits for them, and re-layouts, local(): jnp.take(source.reshape(tok_rows, local_blocks, BLK), local_ids, axis=1)  12.8 us
  transfers between devices with their start and end apart: 10, of which 3 were waited for; matrix products, arithmetic and copies ran while one was open for 39% of the time, Pallas kernels for 0%

profile of v1, /device:TPU:0, one launch (start us, length us, event | category | flops | bytes accessed | tf_op | source)
XLA Modules:
  0.0 474.6 jit_solution(8639758018211684514)
XLA Ops:
  20.2 6.3 %reshape.62 = bf16[28,128,4,128]{3,2,1,0:T(4,128)(2,1)} reshape(bf16[3584,512]{1,0:T(8,128)(2,1)} %param.9) | data formatting | bytes 7340032 | tf_op jit(solution)/shard_map/reshape | solution.py:35
  29.4 61.9 %all-reduce.1 = bf16[512,256]{1,0:T(8,128)(2,1)} all-reduce(f32[512,256]{1,0:T(8,128)S(1)} %fusion.36), channel_id=1, replica_groups=mesh['feat'=8,'seq'=16] {'feat'}, use_global_device_ids=true, to_apply=%region_0.2 | all-reduce | flops 131072 | bytes 786432 | tf_op jit(solution)/shard_map/psum | solution.py:46
  100.4 4.2 gather_fusion.3
  107.5 5.8 %select_bitcast_fusion = (bf16[512,28,1,128]{3,0,2,1:T(8,128)(2,1)S(1)}, bf16[512,28,1,128]{3,0,2,1:T(8,128)(2,1)}) fusion(bf16[28,512,128]{2,1,0:T(8,128)(2,1)} %gather_fusion.3, pred[28]{0:T(512)(128)(4,1)S(1)} %get-tuple-element.46, bf16[28,512,128]{2,1,0:T(8,128)(2,1)} %gather_fusion.2, pred[28]{0:T(512)(128)(4,1)S(1)} %get-tuple-element.48), kind=kLoop, calls=%fused_computation.32 | loop fusion | flops 3670016 | bytes 14680120 | tf_op jit(solution)/shard_map/stack | solution.py:43
  113.5 4.1 select_bitcast_fusion.2
  118.2 9.7 %fusion.11 = f32[28,512,128,1]{1,2,3,0:T(8,128)} fusion(bf16[28,128,4,128]{3,2,1,0:T(4,128)(2,1)S(1)} %copy-done.5, bf16[512,28,1,128]{3,0,2,1:T(8,128)(2,1)S(1)} %get-tuple-element.50, bf16[512,28,1,128]{3,0,2,1:T(8,128)(2,1)} %get-tuple-element.51, bf16[512,28,1,128]{3,0,2,1:T(8,128)(2,1)} %get-tuple-element.52, ...), kind=kOutput, calls=%fused_computation.38 | convolution fusion | flops 1901068288 | bytes 25690112 | tf_op jit(solution)/shard_map/tfli,foli->tfo/dot_general | solution.py:44
  127.9 8.5 %copy.63 = f32[512,3584]{1,0:T(8,128)} copy(f32[512,3584]{0,1:T(8,128)} %bitcast.129) | data formatting | bytes 14680064 | tf_op jit(solution)/shard_map/reshape | solution.py:47
  136.4 10.3 %fusion.2 = (bf16[512,3584]{1,0:T(8,128)(2,1)S(1)}, bf16[512,3584]{1,0:T(8,128)(2,1)}) fusion(bf16[512,3584]{1,0:T(8,128)(2,1)} %param.13, f32[512,3584]{1,0:T(8,128)} %copy.63, bf16[512,256]{1,0:T(8,128)(2,1)S(1)} %copy-done.10, bf16[3584,256]{1,0:T(8,128)(2,1)S(1)} %copy-done), kind=kOutput, calls=%fused_computation.16 | convolution fusion | flops 983564288 | bytes 20447232 | tf_op jit(solution)/shard_map/tr,or->to/dot_general | solution.py:47
  150.5 5.0 %convolution_multiply_fusion = f32[3584,256]{1,0:T(8,128)} fusion(bf16[512,3584]{1,0:T(8,128)(2,1)} %copy-done.7, bf16[512,256]{1,0:T(8,128)(2,1)S(1)} %copy-done.10), kind=kOutput, calls=%fused_computation.31 | convolution fusion | flops 940441600 | bytes 7602176 | tf_op jit(solution)/shard_map/to,tr->or/dot_general | solution.py:83
  155.6 6.0 %copy.64 = bf16[512,3584]{0,1:T(8,128)(2,1)} copy(bf16[512,3584]{1,0:T(8,128)(2,1)} %copy-done.7) | data formatting | bytes 7340032 | tf_op jit(solution)/shard_map/convert_element_type | solution.py:51
  161.6 92.5 %all-gather.3.cloned.1.call-done = f32[4096,256]{1,0:T(8,128)} async-done(((f32[512,256]{1,0:T(8,128)}), f32[4096,256]{1,0:T(8,128)}) %all-gather.3.cloned.1.call-update) | async-done | bytes 4194320 | tf_op jit(solution)/shard_map/all_gather | solution.py:53
  258.5 10.4 %broadcast_multiply_fusion = f32[28,128,4,128]{3,1,2,0:T(8,128)} fusion(bf16[512,28,128,1]{0,2,3,1:T(8,128)(2,1)} %bitcast.127, bf16[512,28,1,128]{3,0,2,1:T(8,128)(2,1)} %copy-done.8, bf16[512,28,1,128]{3,0,2,1:T(8,128)(2,1)} %get-tuple-element.51, bf16[512,28,1,128]{3,0,2,1:T(8,128)(2,1)} %get-tuple-element.52, ...), kind=kOutput, calls=%fused_computation.36 | convolution fusion | flops 1939603456 | bytes 25690112 | tf_op jit(solution)/shard_map/tfo,tfli->foli/dot_general | solution.py:79
  268.9 9.2 %copy.72 = f32[28,128,4,128]{3,2,1,0:T(4,128)S(1)} copy(f32[28,128,4,128]{3,1,2,0:T(8,128)} %broadcast_multiply_fusion) | data formatting | bytes 14680064 | tf_op jit(solution)/shard_map/mul | solution.py:80
  282.0 17.0 %convolution_bitcast_fusion = f32[512,28,4,128]{3,0,2,1:T(8,128)} fusion(bf16[512,28,128,1]{0,2,3,1:T(8,128)(2,1)} %bitcast.128, bf16[28,128,4,128]{3,2,1,0:T(4,128)(2,1)} %reshape.62), kind=kOutput, calls=%fused_computation.9 | convolution fusion | flops 1879048192 | bytes 36700160 | tf_op jit(solution)/shard_map/tfo,foli->tfli/dot_general | solution.py:59
  299.0 20.2 %slice_bitcast_fusion.3 = (f32[28,512,128]{2,1,0:T(8,128)}, f32[28,512,128]{2,1,0:T(8,128)}, f32[28,512,128]{2,1,0:T(8,128)}, f32[28,512,128]{2,1,0:T(8,128)}) fusion(f32[512,28,4,128]{3,0,2,1:T(8,128)} %convolution_bitcast_fusion), kind=kLoop, calls=%fused_computation.28 | loop fusion | bytes 58720256 | tf_op jit(solution)/shard_map/squeeze | solution.py:69
  320.7 17.5 %scatter_fusion.1 = f32[512,8,128]{2,0,1:T(8,128)} fusion(f32[512,8,128]{2,0,1:T(8,128)} %broadcast.93.clone.2, s32[28]{0:T(128)S(1)} %get-tuple-element.41, f32[28,512,128]{2,1,0:T(8,128)} %get-tuple-element.37), kind=kCustom, calls=%fused_computation.5 | custom fusion | flops 1835008 | bytes 22020208 | tf_op jit(solution)/shard_map/scatter-add | solution.py:69
  341.4 3.8 collective-permute-start.3
  346.8 18.5 %scatter_fusion.2 = f32[512,8,128]{2,0,1:T(8,128)} fusion(f32[512,8,128]{2,0,1:T(8,128)} %broadcast.93.clone.1, s32[28]{0:T(128)S(1)} %get-tuple-element.42, f32[28,512,128]{2,1,0:T(8,128)} %get-tuple-element.36), kind=kCustom, calls=%fused_computation.6 | custom fusion | flops 1835008 | bytes 22020208 | tf_op jit(solution)/shard_map/scatter-add | solution.py:69
  370.0 17.8 %scatter_fusion.3 = f32[512,8,128]{2,0,1:T(8,128)} fusion(f32[512,8,128]{2,0,1:T(8,128)} %broadcast.93.clone, s32[28]{0:T(128)S(1)} %get-tuple-element.43, f32[28,512,128]{2,1,0:T(8,128)} %get-tuple-element.35), kind=kCustom, calls=%fused_computation.7 | custom fusion | flops 1835008 | bytes 22020208 | tf_op jit(solution)/shard_map/scatter-add | solution.py:69
  392.5 18.2 %scatter_fusion = f32[512,8,128]{2,0,1:T(8,128)} fusion(f32[512,8,128]{2,0,1:T(8,128)} %broadcast.93.clone.3, s32[28]{0:T(128)S(1)} %get-tuple-element.40, f32[28,512,128]{2,1,0:T(8,128)} %get-tuple-element.34), kind=kCustom, calls=%fused_computation.4 | custom fusion | flops 1835008 | bytes 22020208 | tf_op jit(solution)/shard_map/scatter-add | solution.py:69
  410.6 24.8 %collective-permute-done.4 = f32[512,1024]{1,0:T(8,128)} collective-permute-done((f32[512,1024]{1,0:T(8,128)}, f32[512,1024]{1,0:T(8,128)}, u32[]{:S(2)}, u32[]{:S(2)}) %collective-permute-start.4) | collective-permute-done | bytes 2097184 | tf_op jit(solution)/shard_map/ppermute | solution.py:15
  435.4 7.5 %collective-permute-done.5 = f32[512,1024]{1,0:T(8,128)} collective-permute-done((f32[512,1024]{1,0:T(8,128)}, f32[512,1024]{1,0:T(8,128)}, u32[]{:S(2)}, u32[]{:S(2)}) %collective-permute-start.5) | collective-permute-done | bytes 2097184 | tf_op jit(solution)/shard_map/ppermute | solution.py:15
  443.0 4.2 fusion.16
  447.2 18.0 %all_to_all.16 = bf16[8,64,1024]{2,1,0:T(8,128)(2,1)S(1)} all-to-all(bf16[8,64,1024]{2,1,0:T(8,128)(2,1)S(1)} %bitcast.130), channel_id=1, replica_groups=mesh['feat'=8,'seq'=16] {'feat'}, dimensions={0} | all-to-all | bytes 2097152 | tf_op jit(solution)/shard_map/all_to_all | solution.py:76
  (73 shorter events, 57.2 us)
Async XLA Ops:
  8.0 128.4 %copy-start = (bf16[3584,256]{1,0:T(8,128)(2,1)S(1)}, bf16[3584,256]{1,0:T(8,128)(2,1)}, u32[]{:S(2)}) copy-start(bf16[3584,256]{1,0:T(8,128)(2,1)} %param.10) | copy-start | bytes 5505028
  8.0 10.5 %copy-start.11 = (s32[28,4]{0,1:T(4,128)S(1)}, s32[28,4]{0,1:T(4,128)}, u32[]{:S(2)}) copy-start(s32[28,4]{0,1:T(4,128)} %param.12) | copy-start | bytes 1348
  8.0 246.1 %all-gather.3.cloned.1.call-start = ((), (), s32[]{:S(2)}) async-start(), calls=%async_computation.6 | async-start | bytes 4718592 | tf_op jit(solution)/shard_map/all_gather | solution.py:53
  10.5 80.8 %collective-permute-start.1 = (bf16[512,1024]{0,1:T(8,128)(2,1)}, bf16[512,1024]{0,1:T(8,128)(2,1)}, u32[]{:S(2)}, u32[]{:S(2)}) collective-permute-start(bf16[512,1024]{0,1:T(8,128)(2,1)} %copy.54), channel_id=1, source_target_pairs={{0,32},{16,48},{32,0},{48,16},{64,96},{80,112},{96,64},{112,80},{1... | collective-permute-start | bytes 3145736 | tf_op jit(solution)/shard_map/ppermute | solution.py:15
  12.0 80.9 %collective-permute-start.2 = (bf16[512,1024]{0,1:T(8,128)(2,1)}, bf16[512,1024]{0,1:T(8,128)(2,1)}, u32[]{:S(2)}, u32[]{:S(2)}) collective-permute-start(bf16[512,1024]{0,1:T(8,128)(2,1)} %copy.54), channel_id=1, source_target_pairs={{0,16},{16,0},{32,48},{48,32},{64,80},{80,64},{96,112},{112,96},{1... | collective-permute-start | bytes 3145736 | tf_op jit(solution)/shard_map/ppermute | solution.py:15
  14.0 81.3 %collective-permute-start = (bf16[512,1024]{0,1:T(8,128)(2,1)}, bf16[512,1024]{0,1:T(8,128)(2,1)}, u32[]{:S(2)}, u32[]{:S(2)}) collective-permute-start(bf16[512,1024]{0,1:T(8,128)(2,1)} %copy.54), channel_id=1, source_target_pairs={{0,64},{16,80},{32,96},{48,112},{64,0},{80,16},{96,32},{112,48},{1... | collective-permute-start | bytes 3145736 | tf_op jit(solution)/shard_map/ppermute | solution.py:15
  100.4 4.2 copy-start.2
  107.5 5.8 %copy-start.3 = (bf16[28,512,128]{2,1,0:T(8,128)(2,1)S(1)}, bf16[28,512,128]{2,1,0:T(8,128)(2,1)}, u32[]{:S(2)}) copy-start(bf16[28,512,128]{2,1,0:T(8,128)(2,1)} %gather_fusion) | copy-start | bytes 11010052
  107.5 6.0 %copy-start.4 = (bf16[28,512,128]{2,1,0:T(8,128)(2,1)S(1)}, bf16[28,512,128]{2,1,0:T(8,128)(2,1)}, u32[]{:S(2)}) copy-start(bf16[28,512,128]{2,1,0:T(8,128)(2,1)} %gather_fusion.1) | copy-start | bytes 11010052
  113.3 4.9 %copy-start.8 = (bf16[512,28,1,128]{3,0,2,1:T(8,128)(2,1)}, bf16[512,28,1,128]{3,0,2,1:T(8,128)(2,1)S(1)}, u32[]{:S(2)}) copy-start(bf16[512,28,1,128]{3,0,2,1:T(8,128)(2,1)S(1)} %get-tuple-element.50) | copy-start | bytes 11010052
  113.5 4.8 %copy-start.5 = (bf16[28,128,4,128]{3,2,1,0:T(4,128)(2,1)S(1)}, bf16[28,128,4,128]{3,2,1,0:T(4,128)(2,1)}, u32[]{:S(2)}) copy-start(bf16[28,128,4,128]{3,2,1,0:T(4,128)(2,1)} %reshape.62) | copy-start | bytes 11010052
  127.9 8.5 %copy-start.10 = (bf16[512,256]{1,0:T(8,128)(2,1)S(1)}, bf16[512,256]{1,0:T(8,128)(2,1)}, u32[]{:S(2)}) copy-start(bf16[512,256]{1,0:T(8,128)(2,1)} %all-reduce.1) | copy-start | bytes 786436
  146.7 1.8 copy-start.7
  150.5 316.6 %reduce-scatter.8.cloned.1.call-start = ((), (), s32[]{:S(2)}) async-start(), calls=%async_computation.5 | async-start | bytes 3899392 | tf_op jit(solution)/shard_map/reduce_scatter | solution.py:90
  155.6 311.4 %reduce-scatter.10.cloned.1.call-start = ((), (), s32[]{:S(2)}) async-start(), calls=%async_computation.7 | async-start | bytes 1114112
  161.6 95.0 %copy-start.6 = (bf16[512,1024]{1,0:T(8,128)(2,1)S(1)}, bf16[512,1024]{1,0:T(8,128)(2,1)}, u32[]{:S(2)}) copy-start(bf16[512,1024]{1,0:T(8,128)(2,1)} %param.8) | copy-start | bytes 3145732
  258.4 208.6 %reduce-scatter.6.cloned.1.call-start = ((), (), s32[]{:S(2)}) async-start(), calls=%async_computation.4 | async-start | bytes 7798784 | tf_op jit(solution)/shard_map/reduce_scatter | solution.py:81
  341.4 69.2 %collective-permute-start.3 = (f32[512,1024]{1,0:T(8,128)}, f32[512,1024]{1,0:T(8,128)}, u32[]{:S(2)}, u32[]{:S(2)}) collective-permute-start(f32[512,1024]{1,0:T(8,128)} %copy_bitcast_fusion.3), channel_id=1, source_target_pairs={{0,64},{16,80},{32,96},{48,112},{64,0},{80,16},{96,32},{112,48},{1... | collective-permute-start | bytes 6291464 | tf_op jit(solution)/shard_map/ppermute | solution.py:15
  368.5 67.0 %collective-permute-start.4 = (f32[512,1024]{1,0:T(8,128)}, f32[512,1024]{1,0:T(8,128)}, u32[]{:S(2)}, u32[]{:S(2)}) collective-permute-start(f32[512,1024]{1,0:T(8,128)} %copy_bitcast_fusion.2), channel_id=1, source_target_pairs={{0,32},{16,48},{32,0},{48,16},{64,96},{80,112},{96,64},{112,80},{1... | collective-permute-start | bytes 6291464 | tf_op jit(solution)/shard_map/ppermute | solution.py:15
  391.0 52.0 %collective-permute-start.5 = (f32[512,1024]{1,0:T(8,128)}, f32[512,1024]{1,0:T(8,128)}, u32[]{:S(2)}, u32[]{:S(2)}) collective-permute-start(f32[512,1024]{1,0:T(8,128)} %copy_bitcast_fusion.1), channel_id=1, source_target_pairs={{0,16},{16,0},{32,48},{48,32},{64,80},{80,64},{96,112},{112,96},{1... | collective-permute-start | bytes 6291464 | tf_op jit(solution)/shard_map/ppermute | solution.py:15
  392.5 50.5 %copy-start.9 = (bf16[1024,256]{1,0:T(8,128)(2,1)S(1)}, bf16[1024,256]{1,0:T(8,128)(2,1)}, u32[]{:S(2)}) copy-start(bf16[1024,256]{1,0:T(8,128)(2,1)} %param.11) | copy-start | bytes 1572868
  443.0 24.1 %copy-start.1 = (bf16[3584,256]{1,0:T(8,128)(2,1)S(1)}, bf16[3584,256]{1,0:T(8,128)(2,1)}, u32[]{:S(2)}) copy-start(bf16[3584,256]{1,0:T(8,128)(2,1)} %param.10) | copy-start | bytes 5505028
Sparse Core Ops, SparseCore 0:
  150.6 103.4 all-gather.2
Sparse Core Ops, SparseCore 1:
  155.7 98.3 reduce-scatter.7
  258.5 69.6 reduce-scatter.9
  333.4 98.0 reduce-scatter.5
